TPU v7x, 128 devices: a whole 4x4x4 slice. The times are simulated.
128 devices in a mesh: dp: 16 (over y, x), seq: 8 (over z, core).
Axes of the slice: x: 4, y: 4, z: 4, core: 2. Of those that a mesh axis runs over, the one named last changes fastest.
Arguments:
- feats: bfloat16 [65536, 1024], P(('dp', 'seq')), may hold values from -6 to 6
- gain: float32 [1024], replicated, may hold values from 0.1 to 1.9
- w_qkv: bfloat16 [1024, 3072], replicated, as said below
- w_out: bfloat16 [1024, 1024], replicated, may hold values from -3 to 3
- block_cols: int32 [16, 32, 8], P('dp'), may hold values from 0 to 31, as said below
- block_counts: int32 [16, 32], P('dp'), may hold values from 1 to 8, 128 in all within a row
- cotan: bfloat16 [65536, 1024], P(('dp', 'seq')), may hold values from -0.3984375 to 0.3984375
Outputs:
- result: bfloat16 [65536, 1024], P(('dp', 'seq'))
- grad_feats: bfloat16 [65536, 1024], P(('dp', 'seq'))
- grad_qkv: bfloat16 [1024, 3072], P('seq')
- grad_out: bfloat16 [1024, 1024], P('seq')
Inputs may be any that keep to these rules, and one draw needn't show every extreme that they name: `block_cols`: for every batch and row block r, the 8 listed column blocks are distinct and the first is r itself. `block_counts`: each batch's counts sum to 128. `w_qkv`: entries lie within 70 / sqrt(1024) in magnitude.
All inputs are finite; a program needn't handle non-finite values.
Results may differ from a plain program's by a relative error of at most 0.014.
Values may be sent and summed in bfloat16 or wider, within the bound.
A program may use at most 128 MiB of HBM per device.

v0:
```python
import jax
import jax.numpy as jnp
from jax import lax
from jax.sharding import PartitionSpec as P

HD = 64
BLK = 128
MAXB = 8
EPSILON = 1e-05


def layer_norm(feats, gain):
    values_f = feats.astype(jnp.float32)
    centred = values_f - jnp.mean(values_f, axis=1, keepdims=True)
    inverse = lax.rsqrt(jnp.mean(centred * centred, axis=1, keepdims=True) + EPSILON)
    scaled = centred * inverse
    return (scaled, inverse, (scaled * gain[None, :]).astype(jnp.bfloat16))


def live_slots(counts):
    return jnp.arange(MAXB, dtype=jnp.int32)[None, :] < counts[:, None]


def contract_rows(left_cols, right_cols):
    return lax.dot_general(
        left_cols, right_cols, (((0,), (0,)), ((), ())), preferred_element_type=jnp.float32
    )


def stacked_table(key_heads, value_heads, block_total, head_count):
    key_b = key_heads.reshape(block_total, BLK, head_count, HD)
    value_b = value_heads.reshape(block_total, BLK, head_count, HD)
    return jnp.concatenate([key_b, value_b], axis=3).reshape(block_total, BLK * head_count * 2 * HD)


def select_blocks(onehot, table, head_count):
    picked = jnp.einsum("gsc,cf->gsf", onehot, table, preferred_element_type=jnp.float32).astype(
        jnp.bfloat16
    )
    picked = picked.reshape(onehot.shape[0], onehot.shape[1], BLK, head_count, 2 * HD)
    return (picked[..., :HD], picked[..., HD:])


def forward_blocks(query_heads, key_heads, value_heads, col_blocks, counts, head_count):
    per_step = 4
    block_total = query_heads.shape[0] // BLK
    steps_count = block_total // per_step
    query_b = query_heads.reshape(steps_count, per_step, BLK, head_count, HD)
    table = stacked_table(key_heads, value_heads, block_total, head_count)
    col_steps = col_blocks.reshape(steps_count, per_step, MAXB)
    count_steps = counts.reshape(steps_count, per_step)
    block_range = jnp.arange(block_total, dtype=jnp.int32)
    score_scale = HD ** (-0.5)

    def forward_block_step(inputs):
        query_g, col_g, count_g = inputs
        onehot = (col_g[:, :, None] == block_range[None, None, :]).astype(jnp.bfloat16)
        key_g, value_g = select_blocks(onehot, table, head_count)
        scores = (
            jnp.einsum("gqhd,gskhd->ghqsk", query_g, key_g, preferred_element_type=jnp.float32)
            * score_scale
        )
        live_mask = live_slots(count_g)[:, None, None, :, None]
        row_max = jnp.max(jnp.where(live_mask, scores, -jnp.inf), axis=(3, 4), keepdims=True)
        row_total = jnp.sum(
            jnp.where(live_mask, jnp.exp(scores - row_max), 0.0), axis=(3, 4), keepdims=True
        )
        log_total = row_max + jnp.log(row_total)
        probabilities = jnp.where(live_mask, jnp.exp(scores - log_total), 0.0).astype(jnp.bfloat16)
        attended = jnp.einsum(
            "ghqsk,gskhd->gqhd", probabilities, value_g, preferred_element_type=jnp.float32
        )
        return (attended.astype(jnp.bfloat16), log_total[:, :, :, 0, 0])

    attended, log_total = lax.map(forward_block_step, (query_b, col_steps, count_steps))
    return (attended.reshape(query_heads.shape), log_total)


def backward_blocks(
    query_heads,
    key_heads,
    value_heads,
    attended_heads,
    grad_heads,
    log_total,
    col_blocks,
    counts,
    head_count,
):
    per_step = 4
    block_total = query_heads.shape[0] // BLK
    steps_count = block_total // per_step
    query_b = query_heads.reshape(steps_count, per_step, BLK, head_count, HD)
    grad_b = grad_heads.reshape(steps_count, per_step, BLK, head_count, HD)
    attended_b = attended_heads.reshape(steps_count, per_step, BLK, head_count, HD)
    table = stacked_table(key_heads, value_heads, block_total, head_count)
    col_steps = col_blocks.reshape(steps_count, per_step, MAXB)
    count_steps = counts.reshape(steps_count, per_step)
    delta_all = jnp.sum(attended_b.astype(jnp.float32) * grad_b.astype(jnp.float32), axis=4)
    block_range = jnp.arange(block_total, dtype=jnp.int32)
    score_scale = HD ** (-0.5)

    def backward_block_step(carry, inputs):
        key_sum, value_sum = carry
        query_g, grad_g, delta_g, log_g, col_g, count_g = inputs
        matches = col_g[:, :, None] == block_range[None, None, :]
        key_g, value_g = select_blocks(matches.astype(jnp.bfloat16), table, head_count)
        scores = (
            jnp.einsum("gqhd,gskhd->ghqsk", query_g, key_g, preferred_element_type=jnp.float32)
            * score_scale
        )
        live_mask = live_slots(count_g)[:, None, None, :, None]
        probabilities = jnp.where(
            live_mask, jnp.exp(scores - log_g[:, :, :, None, None]), 0.0
        ).astype(jnp.bfloat16)
        prob_grad = jnp.einsum(
            "gqhd,gskhd->ghqsk", grad_g, value_g, preferred_element_type=jnp.float32
        )
        delta_t = jnp.transpose(delta_g, (0, 2, 1))[:, :, :, None, None]
        score_grad = (
            probabilities.astype(jnp.float32) * (prob_grad - delta_t) * score_scale
        ).astype(jnp.bfloat16)
        query_grad = jnp.einsum(
            "ghqsk,gskhd->gqhd", score_grad, key_g, preferred_element_type=jnp.float32
        ).astype(jnp.bfloat16)
        key_pairs = jnp.einsum(
            "ghqsk,gqhd->gskhd", score_grad, query_g, preferred_element_type=jnp.float32
        )
        value_pairs = jnp.einsum(
            "ghqsk,gqhd->gskhd", probabilities, grad_g, preferred_element_type=jnp.float32
        )
        selector = matches.astype(jnp.float32)
        key_sum = key_sum + jnp.einsum(
            "gsc,gskhd->ckhd", selector, key_pairs, precision=lax.Precision.HIGHEST
        )
        value_sum = value_sum + jnp.einsum(
            "gsc,gskhd->ckhd", selector, value_pairs, precision=lax.Precision.HIGHEST
        )
        return ((key_sum, value_sum), query_grad)

    zeros_f = jnp.zeros((block_total, BLK, head_count, HD), jnp.float32)
    (key_sum, value_sum), query_grad = lax.scan(
        backward_block_step,
        (zeros_f, zeros_f),
        (query_b, grad_b, delta_all, log_total, col_steps, count_steps),
    )
    shape = query_heads.shape
    return (
        query_grad.reshape(shape),
        key_sum.reshape(shape).astype(jnp.bfloat16),
        value_sum.reshape(shape).astype(jnp.bfloat16),
    )


def body(feats, gain, w_qkv, w_out, block_cols, block_counts, cotan):
    seq_count = lax.axis_size("seq")
    model_width = feats.shape[1]
    qkv_width = 3 * model_width
    scaled, inverse, normed = layer_norm(feats, gain)
    mixed_proj = jnp.dot(normed, w_qkv, preferred_element_type=jnp.float32).astype(jnp.bfloat16)
    query_rows = mixed_proj[:, :model_width]
    key_rows = mixed_proj[:, model_width : 2 * model_width]
    value_rows = mixed_proj[:, 2 * model_width :]
    query_heads, key_heads, value_heads = (
        lax.all_to_all(query_rows, "seq", split_axis=1, concat_axis=0, tiled=True),
        lax.all_to_all(key_rows, "seq", split_axis=1, concat_axis=0, tiled=True),
        lax.all_to_all(value_rows, "seq", split_axis=1, concat_axis=0, tiled=True),
    )
    head_count = query_heads.shape[1] // HD
    col_blocks = block_cols[0]
    counts = block_counts[0]
    attended_heads, log_total = forward_blocks(
        query_heads, key_heads, value_heads, col_blocks, counts, head_count
    )
    attended = lax.all_to_all(attended_heads, "seq", split_axis=0, concat_axis=1, tiled=True)
    result = (
        feats.astype(jnp.float32) + jnp.dot(attended, w_out, preferred_element_type=jnp.float32)
    ).astype(jnp.bfloat16)
    grad_att = lax.dot_general(
        cotan, w_out, (((1,), (1,)), ((), ())), preferred_element_type=jnp.float32
    ).astype(jnp.bfloat16)
    grad_heads = lax.all_to_all(grad_att, "seq", split_axis=1, concat_axis=0, tiled=True)
    query_grad, key_grad, value_grad = backward_blocks(
        query_heads,
        key_heads,
        value_heads,
        attended_heads,
        grad_heads,
        log_total,
        col_blocks,
        counts,
        head_count,
    )
    query_back, key_back, value_back = (
        lax.all_to_all(query_grad, "seq", split_axis=0, concat_axis=1, tiled=True),
        lax.all_to_all(key_grad, "seq", split_axis=0, concat_axis=1, tiled=True),
        lax.all_to_all(value_grad, "seq", split_axis=0, concat_axis=1, tiled=True),
    )
    grad_mixed = jnp.concatenate([query_back, key_back, value_back], axis=1)
    grad_normed = lax.dot_general(
        grad_mixed, w_qkv, (((1,), (1,)), ((), ())), preferred_element_type=jnp.float32
    )
    gained = grad_normed * gain[None, :]
    mean_one = jnp.mean(gained, axis=1, keepdims=True)
    mean_two = jnp.mean(gained * scaled, axis=1, keepdims=True)
    grad_feats = (
        cotan.astype(jnp.float32) + inverse * (gained - mean_one - scaled * mean_two)
    ).astype(jnp.bfloat16)
    summed = lax.psum(
        jnp.concatenate(
            [contract_rows(normed, grad_mixed), contract_rows(attended, cotan)], axis=1
        ),
        ("dp", "seq"),
    )
    shard_rows = model_width // seq_count
    own_rows = lax.dynamic_slice_in_dim(summed, lax.axis_index("seq") * shard_rows, shard_rows, 0)
    grad_qkv = own_rows[:, :qkv_width].astype(jnp.bfloat16)
    grad_out = own_rows[:, qkv_width:].astype(jnp.bfloat16)
    return (result, grad_feats, grad_qkv, grad_out)


def solution(mesh):
    in_specs = (
        P(("dp", "seq"), None),
        P(),
        P(),
        P(),
        P("dp", None, None),
        P("dp", None),
        P(("dp", "seq"), None),
    )
    out_specs = (P(("dp", "seq"), None), P(("dp", "seq"), None), P("seq", None), P("seq", None))
    return jax.shard_map(body, mesh=mesh, in_specs=in_specs, out_specs=out_specs, check_vma=False)
```

profile of v0, /device:TPU:0, one launch (start us, length us, event | category | flops | bytes accessed | tf_op | source)
XLA Modules:
  0.0 628.2 jit_solution(8621975070728321357)
XLA Ops:
  4.0 6.7 %convolution_convert_fusion.2 = bf16[512,3072]{1,0:T(8,128)(2,1)S(1)} fusion(bf16[1024,3072]{1,0:T(8,128)(2,1)} %param.13, bf16[512,1024]{1,0:T(8,128)(2,1)S(1)} %copy-done.8, f32[1024]{0:T(1024)S(1)} %copy-done.19, f32[512]{0:T(512)S(1)} %add_rsqrt_fusion, f32[512]{0:T(512)S(1)} %broadcast_multiply_fusion.2), kind=kOutput, calls=%fused_computation.70 | convolution fusion | flops 3225419776 | bytes 10493952 | tf_op jit(solution)/shard_map/dot_general | solution.py:160
  13.7 5.4 all-to-all-start.1
  21.4 13.7 %all-to-all-done.1 = bf16[512,8,128]{0,2,1:T(8,128)(2,1)S(1)} async-done(((bf16[512,8,128]{0,2,1:T(8,128)(2,1)}), bf16[512,8,128]{0,2,1:T(8,128)(2,1)S(1)}, u32[]{:S(2)}, u32[]{:S(2)}) %all-to-all-start.1) | async-done | bytes 1048608 | tf_op jit(solution)/shard_map/all_to_all | solution.py:167
  35.0 4.2 all-to-all-start
  41.6 13.7 %all-to-all-done = bf16[512,8,128]{0,2,1:T(8,128)(2,1)} async-done(((bf16[512,8,128]{0,2,1:T(8,128)(2,1)}), bf16[512,8,128]{0,2,1:T(8,128)(2,1)}, u32[]{:S(2)}, u32[]{:S(2)}) %all-to-all-start) | async-done | bytes 1048608 | tf_op jit(solution)/shard_map/all_to_all | solution.py:166
  55.2 4.2 all-to-all-start.2
  60.9 3.5 convolution_convert_fusion.3
  74.0 3.1 pad_maximum_fusion.2
  77.0 4.7 copy.69
  81.7 4.5 reshape.177
  86.2 5.2 all-to-all-start.4
  94.5 59.6 %while.28 = (s32[]{:T(128)}, bf16[8,4,128,2,64]{2,1,4,3,0:T(4,128)(2,1)S(1)}, f32[8,4,2,128]{3,2,1,0:T(2,128)S(1)}, s32[8,4,8]{2,1,0:T(4,128)S(1)}, bf16[32,3276...) while((s32[]{:T(128)}, ...), condition=%wide.region_5.6_spmd.clone, body=%wide.region_2.5_spmd.clone.sunk | while | flops 348192800 | bytes 23626400 | solution.py:75
  155.3 4.8 all-to-all-start.3
  165.6 239.2 %while.29 = (s32[]{:T(128)}, f32[32,128,2,64]{1,0,3,2:T(8,128)}, f32[32,128,2,64]{1,0,3,2:T(8,128)}, bf16[8,4,128,2,64]{2,1,4,3,0:T(4,128)(2,1)}, s32[8,4,8]{2,1...) while((s32[]{:T(128)}, f32[32,128,2,64]{1,0,3,2:T(8,128)}, ...), condition=%wide.region_8.9_spmd.clone, body=%wide.region_7.8_spmd.clone.sunk | while | flops 1153502208 | bytes 98731120 | solution.py:142
  168.1 3.0 fusion.129
  182.9 5.5 bitcast_add_fusion.4
  189.9 3.5 bitcast_add_fusion.5
  197.4 3.0 fusion.129
  212.2 6.1 bitcast_add_fusion.4
  219.9 3.5 bitcast_add_fusion.5
  227.3 3.0 fusion.129
  242.1 6.1 bitcast_add_fusion.4
  249.8 3.5 bitcast_add_fusion.5
  257.3 3.0 fusion.129
  272.0 6.1 bitcast_add_fusion.4
  279.7 3.5 bitcast_add_fusion.5
  287.2 3.0 fusion.129
  302.0 6.1 bitcast_add_fusion.4
  309.7 3.5 bitcast_add_fusion.5
  317.1 3.0 fusion.129
  331.9 6.1 bitcast_add_fusion.4
  339.6 3.5 bitcast_add_fusion.5
  361.8 6.1 bitcast_add_fusion.4
  369.5 3.5 bitcast_add_fusion.5
  391.8 6.1 bitcast_add_fusion.4
  399.4 3.5 bitcast_add_fusion.5
  410.6 4.8 all-to-all-start.7
  421.3 10.2 %all-to-all-done.7 = bf16[8,512,128]{1,2,0:T(8,128)(2,1)} async-done(((bf16[8,512,128]{1,2,0:T(8,128)(2,1)}), bf16[8,512,128]{1,2,0:T(8,128)(2,1)}, u32[]{:S(2)}, u32[]{:S(2)}) %all-to-all-start.7) | async-done | bytes 1048608 | tf_op jit(solution)/shard_map/all_to_all | solution.py:197
  431.5 4.2 all-to-all-start.6
  437.0 14.7 %all-to-all-done.6 = bf16[8,512,128]{1,2,0:T(8,128)(2,1)} async-done(((bf16[8,512,128]{1,2,0:T(8,128)(2,1)}), bf16[8,512,128]{1,2,0:T(8,128)(2,1)}, u32[]{:S(2)}, u32[]{:S(2)}) %all-to-all-start.6) | async-done | bytes 1048608 | tf_op jit(solution)/shard_map/all_to_all | solution.py:196
  451.7 4.2 all-to-all-start.5
  456.0 4.8 fusion.76
  460.8 3.5 fusion.66
  464.3 7.6 %all-to-all-done.5 = bf16[8,512,128]{1,2,0:T(8,128)(2,1)} async-done(((bf16[8,512,128]{1,2,0:T(8,128)(2,1)}), bf16[8,512,128]{1,2,0:T(8,128)(2,1)}, u32[]{:S(2)}, u32[]{:S(2)}) %all-to-all-start.5) | async-done | bytes 1048608 | tf_op jit(solution)/shard_map/all_to_all | solution.py:195
  471.9 8.9 %multiply_reduce_fusion.1 = (f32[512]{0:T(512)S(1)}, f32[512]{0:T(512)S(1)}, f32[512,1024]{1,0:T(8,128)}) fusion(f32[1024]{0:T(1024)S(1)} %copy-done.20, f32[512]{0:T(512)S(1)} %copy-done.17, f32[512]{0:T(512)S(1)} %copy-done.15, bf16[512,1024]{1,0:T(8,128)(2,1)S(1)} %copy-done.9, bf16[1024,3072]{1,0:T(8,128)(2,1)} %param.13, ...), kind=kOutput, calls=%fused_computation.91 | convolution fusion | flops 3234331648 | bytes 12595200 | tf_op jit(solution)/shard_map/dot_general | solution.py:200
  480.8 5.8 fusion.67
  486.6 6.0 pad_maximum_fusion
  492.7 130.1 %all-reduce.1 = bf16[1024,4096]{1,0:T(8,128)(2,1)} all-reduce(f32[1024,4096]{1,0:T(8,128)} %pad_maximum_fusion), channel_id=1, replica_groups=mesh['dp'=16,'seq'=8] {'dp','seq'}, use_global_device_ids=true, to_apply=%region_11.12 | all-reduce | flops 4194304 | bytes 25165824 | tf_op jit(solution)/shard_map/psum | solution.py:209
  (386 shorter events, 252.1 us)
Async XLA Ops:
  0.6 60.2 %copy-start = (bf16[1024,1024]{1,0:T(8,128)(2,1)S(1)}, bf16[1024,1024]{1,0:T(8,128)(2,1)}, u32[]{:S(2)}) copy-start(bf16[1024,1024]{1,0:T(8,128)(2,1)} %param.14) | copy-start | bytes 6291460
  0.6 3.3 copy-start.8
  0.7 3.3 copy-start.19
  2.3 8.4 %copy-start.14 = (f32[512]{0:T(512)}, f32[512]{0:T(512)S(1)}, u32[]{:S(2)}) copy-start(f32[512]{0:T(512)S(1)} %broadcast_multiply_fusion.2) | copy-start | bytes 6148
  3.9 6.7 %copy-start.16 = (f32[512]{0:T(512)}, f32[512]{0:T(512)S(1)}, u32[]{:S(2)}) copy-start(f32[512]{0:T(512)S(1)} %add_rsqrt_fusion) | copy-start | bytes 6148
  13.7 21.4 %all-to-all-start.1 = ((bf16[512,8,128]{0,2,1:T(8,128)(2,1)}), bf16[512,8,128]{0,2,1:T(8,128)(2,1)S(1)}, u32[]{:S(2)}, u32[]{:S(2)}) async-start(bf16[512,8,128]{0,2,1:T(8,128)(2,1)} %bitcast.208), calls=%async_computation.1 | async-start | bytes 2097152 | tf_op jit(solution)/shard_map/all_to_all | solution.py:167
  35.0 20.2 %all-to-all-start = ((bf16[512,8,128]{0,2,1:T(8,128)(2,1)}), bf16[512,8,128]{0,2,1:T(8,128)(2,1)}, u32[]{:S(2)}, u32[]{:S(2)}) async-start(bf16[512,8,128]{0,2,1:T(8,128)(2,1)} %bitcast.207), calls=%async_computation | async-start | bytes 2097152 | tf_op jit(solution)/shard_map/all_to_all | solution.py:166
  39.3 20.2 %copy-start.18 = (s32[1,32,8]{1,2,0:T(8,128)S(1)}, s32[1,32,8]{1,2,0:T(8,128)}, u32[]{:S(2)}) copy-start(s32[1,32,8]{1,2,0:T(8,128)} %param.15) | copy-start | bytes 3076
  39.3 20.8 %copy-start.21 = (s32[1,32]{1,0:T(1,128)S(1)}, s32[1,32]{1,0:T(1,128)}, u32[]{:S(2)}) copy-start(s32[1,32]{1,0:T(1,128)} %param.16) | copy-start | bytes 388
  55.2 31.0 %all-to-all-start.2 = ((bf16[512,8,128]{0,2,1:T(8,128)(2,1)}), bf16[512,8,128]{0,2,1:T(8,128)(2,1)}, u32[]{:S(2)}, u32[]{:S(2)}) async-start(bf16[512,8,128]{0,2,1:T(8,128)(2,1)} %bitcast.206), calls=%async_computation.2 | async-start | bytes 2097152 | tf_op jit(solution)/shard_map/all_to_all | solution.py:165
  86.2 69.1 %all-to-all-start.4 = ((bf16[512,8,128]{0,2,1:T(8,128)(2,1)}), bf16[512,8,128]{0,2,1:T(8,128)(2,1)}, u32[]{:S(2)}, u32[]{:S(2)}) async-start(bf16[512,8,128]{0,2,1:T(8,128)(2,1)} %bitcast.9), calls=%async_computation.4 | async-start | bytes 2097152 | tf_op jit(solution)/shard_map/all_to_all | solution.py:182
  155.3 255.3 %all-to-all-start.3 = ((bf16[8,512,128]{1,2,0:T(8,128)(2,1)}), bf16[8,512,128]{1,2,0:T(8,128)(2,1)}, u32[]{:S(2)}, u32[]{:S(2)}) async-start(bf16[8,512,128]{1,2,0:T(8,128)(2,1)} %all_to_all.109), calls=%async_computation.3 | async-start | bytes 2097152 | tf_op jit(solution)/shard_map/all_to_all | solution.py:175
  174.0 3.5 copy-start.7
  182.9 5.5 copy-start.4
  189.9 3.5 copy-start.2
  203.4 3.5 copy-start.7
  205.7 2.5 copy-start.3
  212.2 6.1 copy-start.4
  219.9 3.5 copy-start.2
  233.3 3.5 copy-start.7
  242.1 6.1 copy-start.4
  249.8 3.5 copy-start.2
  263.2 3.5 copy-start.7
  272.0 6.1 copy-start.4
  279.7 3.5 copy-start.2
  293.1 3.5 copy-start.7
  302.0 6.1 copy-start.4
  309.7 3.5 copy-start.2
  323.1 3.5 copy-start.7
  331.9 6.1 copy-start.4
  339.6 3.5 copy-start.2
  353.0 3.5 copy-start.7
  361.8 6.1 copy-start.4
  369.5 3.5 copy-start.2
  382.9 3.5 copy-start.7
  391.8 6.1 copy-start.4
  399.4 3.5 copy-start.2
  410.6 20.9 %all-to-all-start.7 = ((bf16[8,512,128]{1,2,0:T(8,128)(2,1)}), bf16[8,512,128]{1,2,0:T(8,128)(2,1)}, u32[]{:S(2)}, u32[]{:S(2)}) async-start(bf16[8,512,128]{1,2,0:T(8,128)(2,1)} %copy.80), calls=%async_computation.7 | async-start | bytes 2097152 | tf_op jit(solution)/shard_map/all_to_all | solution.py:197
  418.7 17.1 %copy-start.10 = (bf16[8,4,128,2,64]{2,1,4,3,0:T(4,128)(2,1)S(1)}, bf16[8,4,128,2,64]{2,1,4,3,0:T(4,128)(2,1)}, u32[]{:S(2)}) copy-start(bf16[8,4,128,2,64]{2,1,4,3,0:T(4,128)(2,1)} %get-tuple-element.113) | copy-start | bytes 3145732
  431.5 20.2 %all-to-all-start.6 = ((bf16[8,512,128]{1,2,0:T(8,128)(2,1)}), bf16[8,512,128]{1,2,0:T(8,128)(2,1)}, u32[]{:S(2)}, u32[]{:S(2)}) async-start(bf16[8,512,128]{1,2,0:T(8,128)(2,1)} %copy.79), calls=%async_computation.6 | async-start | bytes 2097152 | tf_op jit(solution)/shard_map/all_to_all | solution.py:196
  451.7 20.2 %all-to-all-start.5 = ((bf16[8,512,128]{1,2,0:T(8,128)(2,1)}), bf16[8,512,128]{1,2,0:T(8,128)(2,1)}, u32[]{:S(2)}, u32[]{:S(2)}) async-start(bf16[8,512,128]{1,2,0:T(8,128)(2,1)} %all_to_all.116), calls=%async_computation.5 | async-start | bytes 2097152 | tf_op jit(solution)/shard_map/all_to_all | solution.py:195
  456.0 4.8 copy-start.9
  460.8 11.1 %copy-start.15 = (f32[512]{0:T(512)S(1)}, f32[512]{0:T(512)}, u32[]{:S(2)}) copy-start(f32[512]{0:T(512)} %copy-done.14) | copy-start | bytes 6148
  460.8 11.1 %copy-start.17 = (f32[512]{0:T(512)S(1)}, f32[512]{0:T(512)}, u32[]{:S(2)}) copy-start(f32[512]{0:T(512)} %copy-done.16) | copy-start | bytes 6148
  460.8 11.1 %copy-start.20 = (f32[1024]{0:T(1024)S(1)}, f32[1024]{0:T(1024)}, u32[]{:S(2)}) copy-start(f32[1024]{0:T(1024)} %param.12) | copy-start | bytes 12292
  480.8 5.8 copy-start.11
  622.8 3.1 copy-start.12
  622.8 3.1 copy-start.13
  (31 other events, 53.9 us)
where the time goes:
time: 637 us; the launch traced here: 628 us
  matrix products  231 us (36%)
  local copies, waits for them, and re-layouts  138 us (22%)
  blocking collectives  130 us (20%)
  waiting for transfers between devices  59.9 us (9%)
  starting transfers between devices  37.2 us (6%)
  other arithmetic  28.9 us (5%)
    psum x1, blocking collectives, body(): lax.psum(jnp.concatenate([contract_rows(normed, grad_mixed), contract_row...  130 us
    dot_general x8, matrix products, backward_block_step(): jnp.einsum('gsc,gskhd->ckhd', selector, key_pairs, precision=lax.Precisio...  48.1 us
    while x120, local copies, waits for them, and re-layouts  42.8 us
    dot_general x16, matrix products, select_blocks(): jnp.einsum('gsc,cf->gsf', onehot, table, preferred_element_type=jnp.float32)  37.4 us
    slice x16, local copies, waits for them, and re-layouts, select_blocks(): return (picked[..., :HD], picked[..., HD:])  31.4 us
    dot_general x8, matrix products, backward_block_step(): jnp.einsum('gsc,gskhd->ckhd', selector, value_pairs, precision=lax.Precis...  28.1 us
    dot_general x8, matrix products, backward_block_step(): jnp.einsum('ghqsk,gqhd->gskhd', score_grad, query_g, preferred_element_ty...  21.4 us
    dot_general x8, matrix products, backward_block_step(): jnp.einsum('gqhd,gskhd->ghqsk', query_g, key_g, preferred_element_type=jn...  18.3 us
  transfers between devices with their start and end apart: 8, of which 5 were waited for; matrix products, arithmetic and copies ran while one was open for 54% of the time, Pallas kernels for 0%

commit v1 on v0

--- a/solution.py
+++ b/solution.py
@@ -7,6 +7,12 @@
 BLK = 128
 MAXB = 8
 EPSILON = 1e-05
+
+
+def _view_node(local, which_axis, chip_axis):
+    for s in (which_axis, chip_axis):
+        local = lax.psum(local, axis_name=s)
+    return local
 
 
 def layer_norm(feats, gain):
@@ -206,11 +212,12 @@
     grad_feats = (
         cotan.astype(jnp.float32) + inverse * (gained - mean_one - scaled * mean_two)
     ).astype(jnp.bfloat16)
-    summed = lax.psum(
+    summed = _view_node(
         jnp.concatenate(
             [contract_rows(normed, grad_mixed), contract_rows(attended, cotan)], axis=1
         ),
-        ("dp", "seq"),
+        which_axis="seq",
+        chip_axis="dp",
     )
     shard_rows = model_width // seq_count
     own_rows = lax.dynamic_slice_in_dim(summed, lax.axis_index("seq") * shard_rows, shard_rows, 0)

time: 637 us -> 1060 us (1.66)
  blocking collectives: 130 us -> 363 us
  waiting for transfers between devices: 59.9 us -> 233 us
  between operations: 1.36 us -> 14.6 us
    psum x1, blocking collectives: 130 us -> 363 us  [_view_node(): local = lax.psum(local, axis_name=s)]
    psum x0 -> x1, waiting for transfers between devices: none -> 170 us  [_view_node(): local = lax.psum(local, axis_name=s)]
  transfers between devices with their start and end apart: 8 -> 9, of which waited for: 5 -> 6; matrix products, arithmetic and copies ran while one was open for 54% -> 33% of each run, Pallas kernels for 0% -> 0%
where the time goes in v1:
time: 1060 us; the launch traced here: 1050 us
  blocking collectives  363 us (34%)
  waiting for transfers between devices  233 us (22%)
  matrix products  230 us (22%)
  local copies, waits for them, and re-layouts  138 us (13%)
  starting transfers between devices  37.2 us (4%)
  other arithmetic  28.9 us (3%)
  between operations  14.6 us (1%)
    psum x1, blocking collectives, _view_node(): local = lax.psum(local, axis_name=s)  363 us
    psum x1, waiting for transfers between devices, _view_node(): local = lax.psum(local, axis_name=s)  170 us
    dot_general x8, matrix products, backward_block_step(): jnp.einsum('gsc,gskhd->ckhd', selector, key_pairs, precision=lax.Precisio...  48.2 us
    while x120, local copies, waits for them, and re-layouts  42.8 us
    dot_general x16, matrix products, select_blocks(): jnp.einsum('gsc,cf->gsf', onehot, table, preferred_element_type=jnp.float32)  37.4 us
    slice x16, local copies, waits for them, and re-layouts, select_blocks(): return (picked[..., :HD], picked[..., HD:])  31.5 us
    dot_general x8, matrix products, backward_block_step(): jnp.einsum('gsc,gskhd->ckhd', selector, value_pairs, precision=lax.Precis...  28.1 us
    dot_general x8, matrix products, backward_block_step(): jnp.einsum('ghqsk,gqhd->gskhd', score_grad, query_g, preferred_element_ty...  21.4 us
  transfers between devices with their start and end apart: 9, of which 6 were waited for; matrix products, arithmetic and copies ran while one was open for 33% of the time, Pallas kernels for 0%

profile of v1, /device:TPU:0, one launch (start us, length us, event | category | flops | bytes accessed | tf_op | source)
XLA Modules:
  0.0 1046.0 jit_solution(2518111499293829909)
XLA Ops:
  10.5 6.7 convolution_convert_fusion.2
  20.2 5.4 all-to-all-start.1
  27.9 13.7 %all-to-all-done.1 = bf16[512,8,128]{0,2,1:T(8,128)(2,1)S(1)} async-done(((bf16[512,8,128]{0,2,1:T(8,128)(2,1)}), bf16[512,8,128]{0,2,1:T(8,128)(2,1)S(1)}, u32[]{:S(2)}, u32[]{:S(2)}) %all-to-all-start.1) | async-done | bytes 1048608 | tf_op jit(solution)/shard_map/all_to_all | solution.py:173
  41.6 4.2 all-to-all-start
  48.1 13.7 %all-to-all-done = bf16[512,8,128]{0,2,1:T(8,128)(2,1)} async-done(((bf16[512,8,128]{0,2,1:T(8,128)(2,1)}), bf16[512,8,128]{0,2,1:T(8,128)(2,1)}, u32[]{:S(2)}, u32[]{:S(2)}) %all-to-all-start) | async-done | bytes 1048608 | tf_op jit(solution)/shard_map/all_to_all | solution.py:172
  61.8 4.2 all-to-all-start.2
  67.4 3.5 convolution_convert_fusion.3
  80.5 3.1 pad_maximum_fusion.2
  83.5 4.7 copy.69
  88.3 4.5 reshape.177
  92.8 5.2 all-to-all-start.4
  101.0 59.5 %while.28 = (s32[]{:T(128)}, bf16[8,4,128,2,64]{2,1,4,3,0:T(4,128)(2,1)S(1)}, f32[8,4,2,128]{3,2,1,0:T(2,128)S(1)}, s32[8,4,8]{2,1,0:T(4,128)S(1)}, bf16[32,3276...) while((s32[]{:T(128)}, ...), condition=%wide.region_5.6_spmd.clone, body=%wide.region_2.5_spmd.clone.sunk | while | flops 348192800 | bytes 23626400 | solution.py:81
  161.8 4.8 all-to-all-start.3
  172.1 239.4 %while.29 = (s32[]{:T(128)}, f32[32,128,2,64]{1,0,3,2:T(8,128)}, f32[32,128,2,64]{1,0,3,2:T(8,128)}, bf16[8,4,128,2,64]{2,1,4,3,0:T(4,128)(2,1)}, s32[8,4,8]{2,1...) while((s32[]{:T(128)}, f32[32,128,2,64]{1,0,3,2:T(8,128)}, ...), condition=%wide.region_8.9_spmd.clone, body=%wide.region_7.8_spmd.clone.sunk | while | flops 1153502208 | bytes 98731120 | solution.py:148
  174.6 3.0 fusion.129
  189.4 5.5 bitcast_add_fusion.4
  196.4 3.5 bitcast_add_fusion.5
  203.9 3.0 fusion.129
  218.7 6.1 bitcast_add_fusion.4
  226.4 3.5 bitcast_add_fusion.5
  233.9 3.0 fusion.129
  248.6 6.1 bitcast_add_fusion.4
  256.3 3.5 bitcast_add_fusion.5
  263.8 3.0 fusion.129
  278.6 6.1 bitcast_add_fusion.4
  286.3 3.5 bitcast_add_fusion.5
  308.5 6.1 bitcast_add_fusion.4
  316.2 3.5 bitcast_add_fusion.5
  338.5 6.1 bitcast_add_fusion.4
  346.2 3.5 bitcast_add_fusion.5
  368.4 6.1 bitcast_add_fusion.4
  376.1 3.5 bitcast_add_fusion.5
  383.6 3.0 fusion.129
  398.4 6.1 bitcast_add_fusion.4
  406.1 3.5 bitcast_add_fusion.5
  417.2 4.8 all-to-all-start.7
  427.9 10.2 all-to-all-done.7
  438.1 4.2 all-to-all-start.6
  443.6 14.7 %all-to-all-done.6 = bf16[8,512,128]{1,2,0:T(8,128)(2,1)} async-done(((bf16[8,512,128]{1,2,0:T(8,128)(2,1)}), bf16[8,512,128]{1,2,0:T(8,128)(2,1)}, u32[]{:S(2)}, u32[]{:S(2)}) %all-to-all-start.6) | async-done | bytes 1048608 | tf_op jit(solution)/shard_map/all_to_all | solution.py:202
  458.3 4.2 all-to-all-start.5
  462.7 4.8 fusion.76
  467.5 11.0 %all-to-all-done.5 = bf16[8,512,128]{1,2,0:T(8,128)(2,1)} async-done(((bf16[8,512,128]{1,2,0:T(8,128)(2,1)}), bf16[8,512,128]{1,2,0:T(8,128)(2,1)}, u32[]{:S(2)}, u32[]{:S(2)}) %all-to-all-start.5) | async-done | bytes 1048608 | tf_op jit(solution)/shard_map/all_to_all | solution.py:201
  478.6 5.8 fusion.67
  484.4 6.1 pad_maximum_fusion
  490.5 7.5 multiply_reduce_fusion.1
  499.8 3.5 fusion.66
  503.3 169.7 %all-reduce.3.cloned.1.call-done = f32[1024,4096]{1,0:T(8,128)} async-done(((f32[1024,4096]{1,0:T(8,128)}), f32[1024,4096]{1,0:T(8,128)}) %all-reduce.3.cloned.1.call-update) | async-done | bytes 16777232 | tf_op jit(solution)/shard_map/psum | solution.py:14
  673.0 363.0 %all-reduce.4 = bf16[1024,4096]{1,0:T(8,128)(2,1)} all-reduce(f32[1024,4096]{1,0:T(8,128)} %all-reduce.3.cloned.1.call-done), channel_id=1, replica_groups=mesh['dp'=16,'seq'=8] {'dp'}, use_global_device_ids=true, to_apply=%region_12.13 | all-reduce | flops 4194304 | bytes 25165824 | tf_op jit(solution)/shard_map/psum | solution.py:14
  (387 shorter events, 255.1 us)
Async XLA Ops:
  7.2 60.2 %copy-start = (bf16[1024,1024]{1,0:T(8,128)(2,1)S(1)}, bf16[1024,1024]{1,0:T(8,128)(2,1)}, u32[]{:S(2)}) copy-start(bf16[1024,1024]{1,0:T(8,128)(2,1)} %param.14) | copy-start | bytes 6291460
  7.2 3.3 copy-start.8
  7.2 3.3 copy-start.18
  8.8 8.4 copy-start.13
  10.5 6.7 copy-start.15
  20.2 21.4 %all-to-all-start.1 = ((bf16[512,8,128]{0,2,1:T(8,128)(2,1)}), bf16[512,8,128]{0,2,1:T(8,128)(2,1)S(1)}, u32[]{:S(2)}, u32[]{:S(2)}) async-start(bf16[512,8,128]{0,2,1:T(8,128)(2,1)} %bitcast.208), calls=%async_computation.1 | async-start | bytes 2097152 | tf_op jit(solution)/shard_map/all_to_all | solution.py:173
  41.6 20.2 %all-to-all-start = ((bf16[512,8,128]{0,2,1:T(8,128)(2,1)}), bf16[512,8,128]{0,2,1:T(8,128)(2,1)}, u32[]{:S(2)}, u32[]{:S(2)}) async-start(bf16[512,8,128]{0,2,1:T(8,128)(2,1)} %bitcast.207), calls=%async_computation | async-start | bytes 2097152 | tf_op jit(solution)/shard_map/all_to_all | solution.py:172
  45.8 20.2 %copy-start.17 = (s32[1,32,8]{1,2,0:T(8,128)S(1)}, s32[1,32,8]{1,2,0:T(8,128)}, u32[]{:S(2)}) copy-start(s32[1,32,8]{1,2,0:T(8,128)} %param.15) | copy-start | bytes 3076
  45.8 20.8 %copy-start.20 = (s32[1,32]{1,0:T(1,128)S(1)}, s32[1,32]{1,0:T(1,128)}, u32[]{:S(2)}) copy-start(s32[1,32]{1,0:T(1,128)} %param.16) | copy-start | bytes 388
  61.8 31.0 %all-to-all-start.2 = ((bf16[512,8,128]{0,2,1:T(8,128)(2,1)}), bf16[512,8,128]{0,2,1:T(8,128)(2,1)}, u32[]{:S(2)}, u32[]{:S(2)}) async-start(bf16[512,8,128]{0,2,1:T(8,128)(2,1)} %bitcast.206), calls=%async_computation.2 | async-start | bytes 2097152 | tf_op jit(solution)/shard_map/all_to_all | solution.py:171
  92.8 69.0 %all-to-all-start.4 = ((bf16[512,8,128]{0,2,1:T(8,128)(2,1)}), bf16[512,8,128]{0,2,1:T(8,128)(2,1)}, u32[]{:S(2)}, u32[]{:S(2)}) async-start(bf16[512,8,128]{0,2,1:T(8,128)(2,1)} %bitcast.9), calls=%async_computation.4 | async-start | bytes 2097152 | tf_op jit(solution)/shard_map/all_to_all | solution.py:188
  161.8 255.5 %all-to-all-start.3 = ((bf16[8,512,128]{1,2,0:T(8,128)(2,1)}), bf16[8,512,128]{1,2,0:T(8,128)(2,1)}, u32[]{:S(2)}, u32[]{:S(2)}) async-start(bf16[8,512,128]{1,2,0:T(8,128)(2,1)} %all_to_all.109), calls=%async_computation.3 | async-start | bytes 2097152 | tf_op jit(solution)/shard_map/all_to_all | solution.py:181
  180.5 3.5 copy-start.7
  182.8 2.5 copy-start.3
  189.4 5.5 copy-start.4
  196.4 3.5 copy-start.2
  209.8 3.5 copy-start.7
  218.7 6.1 copy-start.4
  226.4 3.5 copy-start.2
  239.8 3.5 copy-start.7
  248.6 6.1 copy-start.4
  256.3 3.5 copy-start.2
  269.8 3.5 copy-start.7
  278.6 6.1 copy-start.4
  286.3 3.5 copy-start.2
  299.7 3.5 copy-start.7
  308.5 6.1 copy-start.4
  316.2 3.5 copy-start.2
  329.7 3.5 copy-start.7
  338.5 6.1 copy-start.4
  346.2 3.5 copy-start.2
  359.6 3.5 copy-start.7
  368.4 6.1 copy-start.4
  376.1 3.5 copy-start.2
  389.6 3.5 copy-start.7
  398.4 6.1 copy-start.4
  406.1 3.5 copy-start.2
  417.2 20.9 %all-to-all-start.7 = ((bf16[8,512,128]{1,2,0:T(8,128)(2,1)}), bf16[8,512,128]{1,2,0:T(8,128)(2,1)}, u32[]{:S(2)}, u32[]{:S(2)}) async-start(bf16[8,512,128]{1,2,0:T(8,128)(2,1)} %copy.80), calls=%async_computation.7 | async-start | bytes 2097152 | tf_op jit(solution)/shard_map/all_to_all | solution.py:203
  425.3 17.1 %copy-start.10 = (bf16[8,4,128,2,64]{2,1,4,3,0:T(4,128)(2,1)S(1)}, bf16[8,4,128,2,64]{2,1,4,3,0:T(4,128)(2,1)}, u32[]{:S(2)}) copy-start(bf16[8,4,128,2,64]{2,1,4,3,0:T(4,128)(2,1)} %get-tuple-element.113) | copy-start | bytes 3145732
  438.1 20.2 %all-to-all-start.6 = ((bf16[8,512,128]{1,2,0:T(8,128)(2,1)}), bf16[8,512,128]{1,2,0:T(8,128)(2,1)}, u32[]{:S(2)}, u32[]{:S(2)}) async-start(bf16[8,512,128]{1,2,0:T(8,128)(2,1)} %copy.79), calls=%async_computation.6 | async-start | bytes 2097152 | tf_op jit(solution)/shard_map/all_to_all | solution.py:202
  458.3 20.2 %all-to-all-start.5 = ((bf16[8,512,128]{1,2,0:T(8,128)(2,1)}), bf16[8,512,128]{1,2,0:T(8,128)(2,1)}, u32[]{:S(2)}, u32[]{:S(2)}) async-start(bf16[8,512,128]{1,2,0:T(8,128)(2,1)} %all_to_all.116), calls=%async_computation.5 | async-start | bytes 2097152 | tf_op jit(solution)/shard_map/all_to_all | solution.py:201
  462.6 210.4 %all-reduce.3.cloned.1.call-start = ((), (), s32[]{:S(2)}) async-start(), calls=%async_computation.8 | async-start | bytes 33554432 | tf_op jit(solution)/shard_map/psum | solution.py:14
  462.6 15.9 %copy-start.9 = (bf16[512,1024]{1,0:T(8,128)(2,1)S(1)}, bf16[512,1024]{1,0:T(8,128)(2,1)}, u32[]{:S(2)}) copy-start(bf16[512,1024]{1,0:T(8,128)(2,1)} %param.11) | copy-start | bytes 3145732
  462.6 15.9 %copy-start.14 = (f32[512]{0:T(512)S(1)}, f32[512]{0:T(512)}, u32[]{:S(2)}) copy-start(f32[512]{0:T(512)} %copy-done.13) | copy-start | bytes 6148
  462.7 15.9 %copy-start.16 = (f32[512]{0:T(512)S(1)}, f32[512]{0:T(512)}, u32[]{:S(2)}) copy-start(f32[512]{0:T(512)} %copy-done.15) | copy-start | bytes 6148
  462.7 15.9 %copy-start.19 = (f32[1024]{0:T(1024)S(1)}, f32[1024]{0:T(1024)}, u32[]{:S(2)}) copy-start(f32[1024]{0:T(1024)} %param.12) | copy-start | bytes 12292
  478.6 5.8 copy-start.11
  490.4 7.6 copy-start.12
  (31 other events, 53.9 us)
Sparse Core Ops, SparseCore 0:
  490.6 182.3 all-reduce.2
